TPU v7x, 512 devices: a whole 4x8x8 slice. The times are simulated.
512 devices in a mesh: bunch: 32 (over y, x), tile: 16 (over z, core).
Axes of the slice: x: 4, y: 8, z: 8, core: 2. Of those that a mesh axis runs over, the one named last changes fastest.
Arguments:
- cell_index: int32 [2, 32, 2, 16384], P(None, 'bunch', None, 'tile'), may hold values from 0 to 255
- charges: bfloat16 [2, 32, 16384], P(None, 'bunch', 'tile'), may hold values from 0.5 to 2
- momenta: float32 [2, 32, 2, 16384], P(None, 'bunch', None, 'tile'), may hold values from -6 to 6
- fill_pattern: int32 [2, 32], P(None, 'bunch'), may hold values 0 or 1
- encounters: int32 [4, 2, 2, 32], P(None, None, None, 'bunch'), may hold values 0 or 1
- green_spectrum: float32 [256, 256], P(None, 'tile'), may hold values from 0.5 to 4
- stop_gain: float32 [4], replicated, may hold values from 0.5 to 2
- parasitic_gain: float32 [4], replicated, may hold values from 0.25 to 1
Outputs:
- kicked: float32 [2, 32, 2, 16384], P(None, 'bunch', None, 'tile')
All inputs are finite; a program needn't handle non-finite values. No bound on the sum of `fill_pattern` or of `encounters` on one device may be relied on, other than what follows from the above.
Results may differ from a plain program's by a relative error of at most 0.0037.
Values may be sent and summed in bfloat16 or wider, within the bound.
A program may use at most 128 MiB of HBM per device.

v0:
```python
import math
import jax
import jax.numpy as jnp
from jax import lax
from jax.sharding import PartitionSpec as P

GRID = 256
STOPS = 4
OFFSET_CELLS = 32


def from_behind(value, axis, steps):
    count = lax.axis_size(axis)
    pairs = [(source, (source + steps) % count) for source in range(count)]
    return lax.ppermute(value, axis, pairs)


def tables(grid):
    positions = jnp.arange(grid, dtype=jnp.int32)
    phases = (positions[:, None] * positions[None, :] % grid).astype(jnp.float32) * (
        2.0 * math.pi / grid
    )
    return (jnp.cos(phases), jnp.sin(phases))


def transform(matrix, operand):
    return jnp.einsum("mi,ibn->mbn", matrix, operand, precision=lax.Precision.HIGHEST)


def shifted_up(operand, amount):
    kept = operand[..., : GRID - amount]
    widths = [(0, 0)] * (operand.ndim - 1) + [(amount, 0)]
    return jnp.pad(kept, widths)


def shifted_down(operand, amount):
    kept = operand[..., amount:]
    widths = [(0, 0)] * (operand.ndim - 1) + [(0, amount)]
    return jnp.pad(kept, widths)


def pick_rows(field_b, rows_p, cols_p):
    row_count = field_b.shape[0]
    inside = (rows_p >= 0) & (rows_p < row_count)
    safe_row = jnp.clip(rows_p, 0, row_count - 1)
    values = field_b[safe_row, :, cols_p].astype(jnp.float32)
    return jnp.where(inside[:, None], values, 0.0).T


def encounter_sum(partners, encounter_marks, stop_gain, parasitic_gain):
    summed = jnp.zeros(partners[0].shape, jnp.float32)
    for stop_number in range(STOPS):
        summed = summed + stop_gain[stop_number] * partners[stop_number].astype(jnp.float32)
        weight = stop_gain[stop_number] * parasitic_gain[stop_number]
        mark_up = encounter_marks[stop_number, 0].astype(jnp.float32)[None, :, None, None]
        following = shifted_up(partners[stop_number + 1].astype(jnp.float32), OFFSET_CELLS)
        summed = summed + weight * mark_up * following
        if stop_number >= 1:
            mark_down = encounter_marks[stop_number, 1].astype(jnp.float32)[None, :, None, None]
            earlier = shifted_down(partners[stop_number - 1].astype(jnp.float32), OFFSET_CELLS)
            summed = summed + weight * mark_down * earlier
    return summed.astype(jnp.bfloat16)


def body(
    cell_index,
    charges,
    momenta,
    fill_pattern,
    encounters,
    green_spectrum,
    stop_gain,
    parasitic_gain,
):
    bunches_here = cell_index.shape[1]
    particles = cell_index.shape[3]
    grid_count = 2 * bunches_here
    tile_count = lax.axis_size("tile")
    tile_rows = GRID // tile_count
    row_of = cell_index[:, :, 0].reshape(grid_count, particles)
    col_of = cell_index[:, :, 1].reshape(grid_count, particles)
    masked = (charges * fill_pattern.astype(jnp.bfloat16)[:, :, None]).reshape(
        grid_count, particles
    )
    columns = jnp.arange(GRID, dtype=jnp.int32)
    block_size = min(1024, particles)
    block_count = particles // block_size
    rows_here = jnp.arange(tile_rows * lax.axis_size("tile"), dtype=jnp.int32)

    def deposit_one_grid(operands):
        rows_p, cols_p, weight_p = operands
        blocks = (
            rows_p.reshape(block_count, block_size),
            cols_p.reshape(block_count, block_size),
            weight_p.reshape(block_count, block_size),
        )

        def add_block(running, block):
            rows_b, cols_b, weight_b = block
            left_hot = jnp.where(
                rows_b[:, None] == rows_here[None, :],
                weight_b[:, None],
                jnp.zeros((), jnp.bfloat16),
            )
            right_hot = (cols_b[:, None] == columns[None, :]).astype(jnp.bfloat16)
            return (
                running
                + jnp.einsum("pr,pc->rc", left_hot, right_hot, preferred_element_type=jnp.float32),
                None,
            )

        start = jnp.zeros((tile_rows * lax.axis_size("tile"), GRID), jnp.float32)
        result, unused = lax.scan(add_block, start, blocks)
        return result

    per_grid = lax.map(deposit_one_grid, (row_of, col_of, masked))
    charge = lax.psum_scatter(
        jnp.transpose(per_grid, (1, 0, 2)), "tile", scatter_dimension=0, tiled=True
    )
    cosine_table, sine_table = tables(GRID)
    real_part = jnp.einsum("rbg,gn->rbn", charge, cosine_table, precision=lax.Precision.HIGHEST)
    imag_part = -jnp.einsum("rbg,gn->rbn", charge, sine_table, precision=lax.Precision.HIGHEST)
    halves = jnp.stack([real_part, imag_part], axis=2)
    first_col = lax.axis_index("tile") * tile_rows
    col_wave = jnp.sin(
        2.0
        * math.pi
        / GRID
        * (first_col + jnp.arange(tile_rows, dtype=jnp.int32)).astype(jnp.float32)
    )
    row_wave = jnp.sin(2.0 * math.pi / GRID * jnp.arange(GRID, dtype=jnp.int32).astype(jnp.float32))
    columns_block = lax.all_to_all(halves, "tile", split_axis=3, concat_axis=0, tiled=True)
    real_in = columns_block[:, :, 0]
    imag_in = columns_block[:, :, 1]
    spec_real = transform(cosine_table, real_in) + transform(sine_table, imag_in)
    spec_imag = transform(cosine_table, imag_in) - transform(sine_table, real_in)
    pot_real = green_spectrum[:, None, :] * spec_real
    pot_imag = green_spectrum[:, None, :] * spec_imag
    outputs = []
    for sine_wave in (row_wave[:, None, None], col_wave[None, None, :]):
        even_part = sine_wave * pot_imag
        odd_part = -sine_wave * pot_real
        outputs.append(transform(cosine_table, even_part) - transform(sine_table, odd_part))
        outputs.append(transform(sine_table, even_part) + transform(cosine_table, odd_part))
    stacked = jnp.stack(outputs, axis=2)
    returned = lax.all_to_all(stacked, "tile", split_axis=0, concat_axis=3, tiled=True)
    inverse_norm = 1.0 / (GRID * GRID)
    field_x = (
        jnp.einsum("rbn,nj->rbj", returned[:, :, 0], cosine_table, precision=lax.Precision.HIGHEST)
        - jnp.einsum("rbn,nj->rbj", returned[:, :, 1], sine_table, precision=lax.Precision.HIGHEST)
    ) * inverse_norm
    field_y = (
        jnp.einsum("rbn,nj->rbj", returned[:, :, 2], cosine_table, precision=lax.Precision.HIGHEST)
        - jnp.einsum("rbn,nj->rbj", returned[:, :, 3], sine_table, precision=lax.Precision.HIGHEST)
    ) * inverse_norm
    fields = jnp.stack([field_x, field_y], axis=2).astype(jnp.bfloat16)
    beam_first = fields[:, :bunches_here]
    beam_second = fields[:, bunches_here:]
    from_above = [beam_second]
    from_below = [beam_first]
    moving_second = beam_second
    moving_first = beam_first
    for offset in range(1, STOPS + 1):
        moving_second = from_behind(moving_second, "bunch", -1)
        moving_first = from_behind(moving_first, "bunch", 1)
        from_above.append(moving_second)
        from_below.append(moving_first)
    total_first = encounter_sum(from_above, encounters[:, 0], stop_gain, parasitic_gain)
    total_second = encounter_sum(from_below, encounters[:, 1], stop_gain, parasitic_gain)
    totals = jnp.concatenate([total_first, total_second], axis=1)

    def add_one_grid(operands):
        field_b, rows_p, cols_p = operands
        return pick_rows(field_b, rows_p, cols_p)

    kick_sum = lax.map(
        add_one_grid,
        (
            jnp.transpose(lax.all_gather(totals, "tile", axis=0, tiled=True), (1, 0, 2, 3)),
            row_of,
            col_of,
        ),
    )
    return momenta + kick_sum.reshape(2, bunches_here, 2, particles)


def solution(mesh):
    in_specs = (
        P(None, "bunch", None, "tile"),
        P(None, "bunch", "tile"),
        P(None, "bunch", None, "tile"),
        P(None, "bunch"),
        P(None, None, None, "bunch"),
        P(None, "tile"),
        P(),
        P(),
    )
    out_specs = P(None, "bunch", None, "tile")
    return jax.shard_map(body, mesh=mesh, in_specs=in_specs, out_specs=out_specs, check_vma=False)
```

profile of v0, /device:TPU:1, one launch (start us, length us, event | category | flops | bytes accessed | tf_op | source)
XLA Modules:
  0.0 271.0 jit_solution(11180594290852846728)
XLA Ops:
  12.2 62.1 %reduce-scatter.2.cloned.1.call-done = f32[16,2,256]{2,0,1:T(8,128)} async-done(((f32[256,2,256]{2,0,1:T(8,128)}), f32[16,2,256]{2,0,1:T(8,128)}) %reduce-scatter.2.cloned.1.call-update) | async-done | bytes 32784 | tf_op jit(solution)/shard_map/reduce_scatter | solution.py:117
  74.2 2.0 convolution_bitcast_fusion.1
  76.2 2.0 fusion.17
  79.9 7.4 %all-to-all-start = ((f32[16,1,1024]{2,1,0:T(1,128)}), f32[16,1,1024]{2,1,0:T(1,128)S(1)}, u32[]{:S(2)}, u32[]{:S(2)}) async-start(f32[16,1,1024]{2,1,0:T(1,128)} %reshape.198), calls=%async_computation.1 | async-start | bytes 131072 | tf_op jit(solution)/shard_map/all_to_all | solution.py:132
  87.4 7.7 %all-to-all-done = f32[16,1,1024]{2,1,0:T(1,128)S(1)} async-done(((f32[16,1,1024]{2,1,0:T(1,128)}), f32[16,1,1024]{2,1,0:T(1,128)S(1)}, u32[]{:S(2)}, u32[]{:S(2)}) %all-to-all-start) | async-done | bytes 65568 | tf_op jit(solution)/shard_map/all_to_all | solution.py:132
  114.7 2.1 reshape.200
  116.8 3.5 %all-to-all-start.1 = ((f32[16,1,2048]{2,1,0:T(1,128)}), f32[16,1,2048]{2,1,0:T(1,128)S(1)}, u32[]{:S(2)}, u32[]{:S(2)}) async-start(f32[16,1,2048]{2,1,0:T(1,128)} %reshape.200), calls=%async_computation.2 | async-start | bytes 262144 | tf_op jit(solution)/shard_map/all_to_all | solution.py:146
  122.2 7.2 %all-to-all-done.1 = f32[16,1,2048]{2,1,0:T(1,128)S(1)} async-done(((f32[16,1,2048]{2,1,0:T(1,128)}), f32[16,1,2048]{2,1,0:T(1,128)S(1)}, u32[]{:S(2)}, u32[]{:S(2)}) %all-to-all-start.1) | async-done | bytes 131104 | tf_op jit(solution)/shard_map/all_to_all | solution.py:146
  137.8 6.6 %collective-permute-start = (bf16[16,1,2,256]{3,0,1,2:T(8,128)(2,1)S(1)}, bf16[16,1,2,256]{3,0,1,2:T(8,128)(2,1)S(1)}, u32[]{:S(2)}, u32[]{:S(2)}) collective-permute-start(bf16[16,1,2,256]{3,0,1,2:T(8,128)(2,1)S(1)} %get-tuple-element.186), channel_id=1, source_target_pairs={{0,496},{16,0},{32,16},{48,32},{64,48},{80,64},{96,80},{112,96},{1... | collective-permute-start | bytes 49160 | tf_op jit(solution)/shard_map/ppermute | solution.py:15
  160.6 6.7 %collective-permute-start.1 = (bf16[16,1,2,256]{3,0,1,2:T(8,128)(2,1)S(1)}, bf16[16,1,2,256]{3,0,1,2:T(8,128)(2,1)S(1)}, u32[]{:S(2)}, u32[]{:S(2)}) collective-permute-start(bf16[16,1,2,256]{3,0,1,2:T(8,128)(2,1)S(1)} %collective-permute-done), channel_id=1, source_target_pairs={{0,496},{16,0},{32,16},{48,32},{64,48},{80,64},{96,80},{112,96},{1... | collective-permute-start | bytes 49160 | tf_op jit(solution)/shard_map/ppermute | solution.py:15
  167.4 1.9 collective-permute-start.5
  169.4 6.7 %collective-permute-start.2 = (bf16[16,1,2,256]{3,0,1,2:T(8,128)(2,1)S(1)}, bf16[16,1,2,256]{3,0,1,2:T(8,128)(2,1)S(1)}, u32[]{:S(2)}, u32[]{:S(2)}) collective-permute-start(bf16[16,1,2,256]{3,0,1,2:T(8,128)(2,1)S(1)} %collective-permute-done.1), channel_id=1, source_target_pairs={{0,496},{16,0},{32,16},{48,32},{64,48},{80,64},{96,80},{112,96},{1... | collective-permute-start | bytes 49160 | tf_op jit(solution)/shard_map/ppermute | solution.py:15
  176.1 1.9 collective-permute-start.6
  178.0 6.7 %collective-permute-start.3 = (bf16[16,1,2,256]{3,0,1,2:T(8,128)(2,1)S(1)}, bf16[16,1,2,256]{3,0,1,2:T(8,128)(2,1)S(1)}, u32[]{:S(2)}, u32[]{:S(2)}) collective-permute-start(bf16[16,1,2,256]{3,0,1,2:T(8,128)(2,1)S(1)} %collective-permute-done.2), channel_id=1, source_target_pairs={{0,496},{16,0},{32,16},{48,32},{64,48},{80,64},{96,80},{112,96},{1... | collective-permute-start | bytes 49160 | tf_op jit(solution)/shard_map/ppermute | solution.py:15
  184.8 1.9 collective-permute-start.7
  186.8 2.5 add_convert_fusion.1
  189.2 3.4 %collective-permute-done.7 = bf16[16,1,2,256]{3,0,1,2:T(8,128)(2,1)S(1)} collective-permute-done((bf16[16,1,2,256]{3,0,1,2:T(8,128)(2,1)S(1)}, bf16[16,1,2,256]{3,0,1,2:T(8,128)(2,1)S(1)}, u32[]{:S(2)}, u32[]{:S(2)}) %collective-permute-start.7) | collective-permute-done | bytes 16416 | tf_op jit(solution)/shard_map/ppermute | solution.py:15
  192.6 2.5 add_convert_fusion
  195.1 18.9 %all_gather.3 = bf16[256,2,2,256]{3,0,1,2:T(8,128)(2,1)S(1)} all-gather(bf16[16,2,2,256]{3,0,1,2:T(8,128)(2,1)S(1)} %pad_maximum_fusion.2), channel_id=1, replica_groups=mesh['bunch'=32,'tile'=16] {'tile'}, dimensions={0}, use_global_device_ids=true | all-gather | bytes 557056 | tf_op jit(solution)/shard_map/all_gather | solution.py:179
  214.0 49.5 %while.29 = (s32[]{:T(128)}, f32[2,2,1024]{2,1,0:T(2,128)S(1)}, s32[2,1024]{1,0:T(2,128)S(1)}, bf16[2,256,2,256]{3,1,0,2:T(8,128)(2,1)S(1)}, s32[2,1024]{1,0:T(2,128)S(1)}, /*index=5*/s32[]{:T(128)}) while((s32[]{:T(128)}, f32[2,2,1024]{2,1,0:T(2,128)S(1)}, s32[2,1024]{1,0:T(2,128)S(1)}, bf16[2,256,2,256]{3,1,0,2:T(8,128)(2,1)S(1)}, ...), condition=%wide.region_4.5_spmd, body=%wide.region_3.4_spmd.sunk | while | flops 19458 | bytes 1128533 | solution.py:176
  214.1 11.9 %copy.94 = bf16[1,256,2,256]{2,3,1,0:T(8,128)(2,1)} copy(bf16[1,256,2,256]{3,1,0,2:T(8,128)(2,1)S(1)} %constant_dynamic-slice_fusion.5) | data formatting | bytes 524288 | tf_op jit(solution)/shard_map/while/body/jit(dynamic_index_in_dim)/dynamic_slice | solution.py:176
  226.0 12.3 %gather_fusion = bf16[1024,2]{1,0:T(8,128)(2,1)S(1)} fusion(bf16[256,2,256]{1,2,0:T(8,128)(2,1)} %bitcast.203, s32[1024]{0:T(1024)S(1)} %bitcast.202), kind=kCustom, calls=%fused_computation.clone.1 | custom fusion | bytes 16384 | tf_op jit(solution)/shard_map/while/body/eval_jaxpr/gather | solution.py:46
  238.9 11.9 %copy.94 = bf16[1,256,2,256]{2,3,1,0:T(8,128)(2,1)} copy(bf16[1,256,2,256]{3,1,0,2:T(8,128)(2,1)S(1)} %constant_dynamic-slice_fusion.5) | data formatting | bytes 524288 | tf_op jit(solution)/shard_map/while/body/jit(dynamic_index_in_dim)/dynamic_slice | solution.py:176
  250.8 12.3 %gather_fusion = bf16[1024,2]{1,0:T(8,128)(2,1)S(1)} fusion(bf16[256,2,256]{1,2,0:T(8,128)(2,1)} %bitcast.203, s32[1024]{0:T(1024)S(1)} %bitcast.202), kind=kCustom, calls=%fused_computation.clone.1 | custom fusion | bytes 16384 | tf_op jit(solution)/shard_map/while/body/eval_jaxpr/gather | solution.py:46
  (99 shorter events, 43.4 us)
Async XLA Ops:
  6.5 96.4 %copy-start.1 = (f32[256,16]{0,1:T(8,128)S(1)}, f32[256,16]{0,1:T(8,128)}, u32[]{:S(2)}) copy-start(f32[256,16]{0,1:T(8,128)} %param.17) | copy-start | bytes 49156
  6.5 113.7 %copy-start.3 = (f32[4]{0:T(128)S(1)}, f32[4]{0:T(128)}, u32[]{:S(2)}) copy-start(f32[4]{0:T(128)} %param.18) | copy-start | bytes 52
  6.5 67.7 %reduce-scatter.2.cloned.1.call-start = ((), (), s32[]{:S(2)}) async-start(), calls=%async_computation.3 | async-start | bytes 557056 | tf_op jit(solution)/shard_map/reduce_scatter | solution.py:117
  10.6 0.8 copy-start
  10.6 133.7 %copy-start.4 = (f32[4]{0:T(128)S(1)}, f32[4]{0:T(128)}, u32[]{:S(2)}) copy-start(f32[4]{0:T(128)} %param.19) | copy-start | bytes 52
  79.9 15.2 %all-to-all-start = ((f32[16,1,1024]{2,1,0:T(1,128)}), f32[16,1,1024]{2,1,0:T(1,128)S(1)}, u32[]{:S(2)}, u32[]{:S(2)}) async-start(f32[16,1,1024]{2,1,0:T(1,128)} %reshape.198), calls=%async_computation.1 | async-start | bytes 131072 | tf_op jit(solution)/shard_map/all_to_all | solution.py:132
  116.8 12.7 %all-to-all-start.1 = ((f32[16,1,2048]{2,1,0:T(1,128)}), f32[16,1,2048]{2,1,0:T(1,128)S(1)}, u32[]{:S(2)}, u32[]{:S(2)}) async-start(f32[16,1,2048]{2,1,0:T(1,128)} %reshape.200), calls=%async_computation.2 | async-start | bytes 262144 | tf_op jit(solution)/shard_map/all_to_all | solution.py:146
  137.8 22.8 %collective-permute-start = (bf16[16,1,2,256]{3,0,1,2:T(8,128)(2,1)S(1)}, bf16[16,1,2,256]{3,0,1,2:T(8,128)(2,1)S(1)}, u32[]{:S(2)}, u32[]{:S(2)}) collective-permute-start(bf16[16,1,2,256]{3,0,1,2:T(8,128)(2,1)S(1)} %get-tuple-element.186), channel_id=1, source_target_pairs={{0,496},{16,0},{32,16},{48,32},{64,48},{80,64},{96,80},{112,96},{1... | collective-permute-start | bytes 49160 | tf_op jit(solution)/shard_map/ppermute | solution.py:15
  158.6 8.8 %collective-permute-start.4 = (bf16[16,1,2,256]{3,0,1,2:T(8,128)(2,1)S(1)}, bf16[16,1,2,256]{3,0,1,2:T(8,128)(2,1)S(1)}, u32[]{:S(2)}, u32[]{:S(2)}) collective-permute-start(bf16[16,1,2,256]{3,0,1,2:T(8,128)(2,1)S(1)} %get-tuple-element.187), channel_id=1, source_target_pairs={{0,16},{16,32},{32,48},{48,64},{64,80},{80,96},{96,112},{112,128},... | collective-permute-start | bytes 49160 | tf_op jit(solution)/shard_map/ppermute | solution.py:15
  160.6 8.8 %collective-permute-start.1 = (bf16[16,1,2,256]{3,0,1,2:T(8,128)(2,1)S(1)}, bf16[16,1,2,256]{3,0,1,2:T(8,128)(2,1)S(1)}, u32[]{:S(2)}, u32[]{:S(2)}) collective-permute-start(bf16[16,1,2,256]{3,0,1,2:T(8,128)(2,1)S(1)} %collective-permute-done), channel_id=1, source_target_pairs={{0,496},{16,0},{32,16},{48,32},{64,48},{80,64},{96,80},{112,96},{1... | collective-permute-start | bytes 49160 | tf_op jit(solution)/shard_map/ppermute | solution.py:15
  167.4 8.8 %collective-permute-start.5 = (bf16[16,1,2,256]{3,0,1,2:T(8,128)(2,1)S(1)}, bf16[16,1,2,256]{3,0,1,2:T(8,128)(2,1)S(1)}, u32[]{:S(2)}, u32[]{:S(2)}) collective-permute-start(bf16[16,1,2,256]{3,0,1,2:T(8,128)(2,1)S(1)} %collective-permute-done.4), channel_id=1, source_target_pairs={{0,16},{16,32},{32,48},{48,64},{64,80},{80,96},{96,112},{112,128},... | collective-permute-start | bytes 49160 | tf_op jit(solution)/shard_map/ppermute | solution.py:15
  169.4 8.7 %collective-permute-start.2 = (bf16[16,1,2,256]{3,0,1,2:T(8,128)(2,1)S(1)}, bf16[16,1,2,256]{3,0,1,2:T(8,128)(2,1)S(1)}, u32[]{:S(2)}, u32[]{:S(2)}) collective-permute-start(bf16[16,1,2,256]{3,0,1,2:T(8,128)(2,1)S(1)} %collective-permute-done.1), channel_id=1, source_target_pairs={{0,496},{16,0},{32,16},{48,32},{64,48},{80,64},{96,80},{112,96},{1... | collective-permute-start | bytes 49160 | tf_op jit(solution)/shard_map/ppermute | solution.py:15
  176.1 8.7 %collective-permute-start.6 = (bf16[16,1,2,256]{3,0,1,2:T(8,128)(2,1)S(1)}, bf16[16,1,2,256]{3,0,1,2:T(8,128)(2,1)S(1)}, u32[]{:S(2)}, u32[]{:S(2)}) collective-permute-start(bf16[16,1,2,256]{3,0,1,2:T(8,128)(2,1)S(1)} %collective-permute-done.5), channel_id=1, source_target_pairs={{0,16},{16,32},{32,48},{48,64},{64,80},{80,96},{96,112},{112,128},... | collective-permute-start | bytes 49160 | tf_op jit(solution)/shard_map/ppermute | solution.py:15
  178.0 8.7 %collective-permute-start.3 = (bf16[16,1,2,256]{3,0,1,2:T(8,128)(2,1)S(1)}, bf16[16,1,2,256]{3,0,1,2:T(8,128)(2,1)S(1)}, u32[]{:S(2)}, u32[]{:S(2)}) collective-permute-start(bf16[16,1,2,256]{3,0,1,2:T(8,128)(2,1)S(1)} %collective-permute-done.2), channel_id=1, source_target_pairs={{0,496},{16,0},{32,16},{48,32},{64,48},{80,64},{96,80},{112,96},{1... | collective-permute-start | bytes 49160 | tf_op jit(solution)/shard_map/ppermute | solution.py:15
  184.8 7.8 %collective-permute-start.7 = (bf16[16,1,2,256]{3,0,1,2:T(8,128)(2,1)S(1)}, bf16[16,1,2,256]{3,0,1,2:T(8,128)(2,1)S(1)}, u32[]{:S(2)}, u32[]{:S(2)}) collective-permute-start(bf16[16,1,2,256]{3,0,1,2:T(8,128)(2,1)S(1)} %collective-permute-done.6), channel_id=1, source_target_pairs={{0,16},{16,32},{32,48},{48,64},{64,80},{80,96},{96,112},{112,128},... | collective-permute-start | bytes 49160 | tf_op jit(solution)/shard_map/ppermute | solution.py:15
  214.0 49.5 %copy-start.2 = (f32[2,1,2,1024]{3,2,1,0:T(2,128)S(1)}, f32[2,1,2,1024]{3,2,1,0:T(2,128)}, u32[]{:S(2)}) copy-start(f32[2,1,2,1024]{3,2,1,0:T(2,128)} %param.14) | copy-start | bytes 49156
Sparse Core Ops, SparseCore 0:
  11.6 62.6 reduce-scatter.1
where the time goes:
time: 272 us; the launch traced here: 271 us
  waiting for transfers between devices  80.5 us (30%)
  local copies, waits for them, and re-layouts  63.1 us (23%)
  starting transfers between devices  45.1 us (17%)
  between operations  27.4 us (10%)
  matrix products  26.5 us (10%)
  blocking collectives  18.9 us (7%)
  other arithmetic  9.5 us (3%)
    reduce_scatter x1, waiting for transfers between devices, body(): lax.psum_scatter(jnp.transpose(per_grid, (1, 0, 2)), 'tile', scatter_dime...  62.1 us
    ppermute x8, starting transfers between devices, from_behind(): return lax.ppermute(value, axis, pairs)  34.3 us
    gather x2, local copies, waits for them, and re-layouts, pick_rows(): values = field_b[safe_row, :, cols_p].astype(jnp.float32)  24.6 us
    dynamic_slice x4, local copies, waits for them, and re-layouts, body(): lax.map(add_one_grid, (jnp.transpose(lax.all_gather(totals, 'tile', axis=...  23.9 us
    all_gather x1, blocking collectives, body(): lax.all_gather(totals, 'tile', axis=0, tiled=True)  18.9 us
    unnamed x12, matrix products  16 us
    all_to_all x1, waiting for transfers between devices, body(): lax.all_to_all(halves, 'tile', split_axis=3, concat_axis=0, tiled=True)  7.72 us
    all_to_all x1, starting transfers between devices, body(): lax.all_to_all(halves, 'tile', split_axis=3, concat_axis=0, tiled=True)  7.36 us
  transfers between devices with their start and end apart: 11, of which 4 were waited for; matrix products, arithmetic and copies ran while one was open for 2% of the time, Pallas kernels for 0%

commit v1 on v0

--- a/solution.py
+++ b/solution.py
@@ -72,6 +72,11 @@
     stop_gain,
     parasitic_gain,
 ):
+
+    def meet_classes_on(vector, row_axis, axis_k):
+        val2 = lax.all_to_all(jnp.stack(lax.axis_size(row_axis) * [vector], axis=0), row_axis, 0, 0)
+        return jnp.concatenate(val2, axis=axis_k)
+
     bunches_here = cell_index.shape[1]
     particles = cell_index.shape[3]
     grid_count = 2 * bunches_here
@@ -175,11 +180,7 @@
 
     kick_sum = lax.map(
         add_one_grid,
-        (
-            jnp.transpose(lax.all_gather(totals, "tile", axis=0, tiled=True), (1, 0, 2, 3)),
-            row_of,
-            col_of,
-        ),
+        (jnp.transpose(meet_classes_on(totals, "tile", 0), (1, 0, 2, 3)), row_of, col_of),
     )
     return momenta + kick_sum.reshape(2, bunches_here, 2, particles)
 

time: 272 us -> 278 us (1.022)
  blocking collectives: 18.9 us -> 0 us
  waiting for transfers between devices: 80.5 us -> 97.7 us
  starting transfers between devices: 45.1 us -> 51.3 us
    all_gather x1 -> x0, blocking collectives: 18.9 us -> none  [body(): lax.all_gather(totals, 'tile', axis=0, tiled=True)]
    all_to_all x0 -> x1, waiting for transfers between devices: none -> 17.3 us  [meet_classes_on(): lax.all_to_all(jnp.stack(lax.axis_size(row_axis) * [vector], axis=0), row...]
    all_to_all x0 -> x1, starting transfers between devices: none -> 6.17 us  [meet_classes_on(): lax.all_to_all(jnp.stack(lax.axis_size(row_axis) * [vector], axis=0), row...]
  transfers between devices with their start and end apart: 11 -> 12, of which waited for: 4 -> 5; matrix products, arithmetic and copies ran while one was open for 2% -> 2% of each run, Pallas kernels for 0% -> 0%
where the time goes in v1:
time: 278 us; the launch traced here: 277 us
  waiting for transfers between devices  97.7 us (35%)
  local copies, waits for them, and re-layouts  64.2 us (23%)
  starting transfers between devices  51.3 us (18%)
  between operations  27.4 us (10%)
  matrix products  26.5 us (10%)
  other arithmetic  9.8 us (4%)
    reduce_scatter x1, waiting for transfers between devices, body(): lax.psum_scatter(jnp.transpose(per_grid, (1, 0, 2)), 'tile', scatter_dime...  62.1 us
    ppermute x8, starting transfers between devices, from_behind(): return lax.ppermute(value, axis, pairs)  34.3 us
    gather x2, local copies, waits for them, and re-layouts, pick_rows(): values = field_b[safe_row, :, cols_p].astype(jnp.float32)  24.7 us
    dynamic_slice x4, local copies, waits for them, and re-layouts, body(): lax.map(add_one_grid, (jnp.transpose(meet_classes_on(totals, 'tile', 0),...  23.9 us
    all_to_all x1, waiting for transfers between devices, meet_classes_on(): lax.all_to_all(jnp.stack(lax.axis_size(row_axis) * [vector], axis=0), row...  17.3 us
    unnamed x12, matrix products  16 us
    all_to_all x1, waiting for transfers between devices, body(): lax.all_to_all(halves, 'tile', split_axis=3, concat_axis=0, tiled=True)  7.72 us
    all_to_all x1, starting transfers between devices, body(): lax.all_to_all(halves, 'tile', split_axis=3, concat_axis=0, tiled=True)  7.36 us
  transfers between devices with their start and end apart: 12, of which 5 were waited for; matrix products, arithmetic and copies ran while one was open for 2% of the time, Pallas kernels for 0%

profile of v1, /device:TPU:1, one launch (start us, length us, event | category | flops | bytes accessed | tf_op | source)
XLA Modules:
  0.0 276.9 jit_solution(11179310995289421112)
XLA Ops:
  12.1 62.1 %reduce-scatter.2.cloned.1.call-done = f32[16,2,256]{2,0,1:T(8,128)} async-done(((f32[256,2,256]{2,0,1:T(8,128)}), f32[16,2,256]{2,0,1:T(8,128)}) %reduce-scatter.2.cloned.1.call-update) | async-done | bytes 32784 | tf_op jit(solution)/shard_map/reduce_scatter | solution.py:122
  74.2 2.0 convolution_bitcast_fusion.1
  76.2 2.0 fusion.17
  79.9 7.4 %all-to-all-start = ((f32[16,1,1024]{2,1,0:T(1,128)}), f32[16,1,1024]{2,1,0:T(1,128)S(1)}, u32[]{:S(2)}, u32[]{:S(2)}) async-start(f32[16,1,1024]{2,1,0:T(1,128)} %reshape.204), calls=%async_computation.1 | async-start | bytes 131072 | tf_op jit(solution)/shard_map/all_to_all | solution.py:137
  87.4 7.7 %all-to-all-done = f32[16,1,1024]{2,1,0:T(1,128)S(1)} async-done(((f32[16,1,1024]{2,1,0:T(1,128)}), f32[16,1,1024]{2,1,0:T(1,128)S(1)}, u32[]{:S(2)}, u32[]{:S(2)}) %all-to-all-start) | async-done | bytes 65568 | tf_op jit(solution)/shard_map/all_to_all | solution.py:137
  114.7 2.1 reshape.206
  116.8 3.5 %all-to-all-start.1 = ((f32[16,1,2048]{2,1,0:T(1,128)}), f32[16,1,2048]{2,1,0:T(1,128)S(1)}, u32[]{:S(2)}, u32[]{:S(2)}) async-start(f32[16,1,2048]{2,1,0:T(1,128)} %reshape.206), calls=%async_computation.2 | async-start | bytes 262144 | tf_op jit(solution)/shard_map/all_to_all | solution.py:151
  122.2 7.2 %all-to-all-done.1 = f32[16,1,2048]{2,1,0:T(1,128)S(1)} async-done(((f32[16,1,2048]{2,1,0:T(1,128)}), f32[16,1,2048]{2,1,0:T(1,128)S(1)}, u32[]{:S(2)}, u32[]{:S(2)}) %all-to-all-start.1) | async-done | bytes 131104 | tf_op jit(solution)/shard_map/all_to_all | solution.py:151
  137.8 6.6 %collective-permute-start = (bf16[16,1,2,256]{3,0,1,2:T(8,128)(2,1)S(1)}, bf16[16,1,2,256]{3,0,1,2:T(8,128)(2,1)S(1)}, u32[]{:S(2)}, u32[]{:S(2)}) collective-permute-start(bf16[16,1,2,256]{3,0,1,2:T(8,128)(2,1)S(1)} %get-tuple-element.176), channel_id=1, source_target_pairs={{0,496},{16,0},{32,16},{48,32},{64,48},{80,64},{96,80},{112,96},{1... | collective-permute-start | bytes 49160 | tf_op jit(solution)/shard_map/ppermute | solution.py:15
  160.7 6.7 %collective-permute-start.1 = (bf16[16,1,2,256]{3,0,1,2:T(8,128)(2,1)S(1)}, bf16[16,1,2,256]{3,0,1,2:T(8,128)(2,1)S(1)}, u32[]{:S(2)}, u32[]{:S(2)}) collective-permute-start(bf16[16,1,2,256]{3,0,1,2:T(8,128)(2,1)S(1)} %collective-permute-done), channel_id=1, source_target_pairs={{0,496},{16,0},{32,16},{48,32},{64,48},{80,64},{96,80},{112,96},{1... | collective-permute-start | bytes 49160 | tf_op jit(solution)/shard_map/ppermute | solution.py:15
  167.5 1.9 collective-permute-start.5
  169.5 6.7 %collective-permute-start.2 = (bf16[16,1,2,256]{3,0,1,2:T(8,128)(2,1)S(1)}, bf16[16,1,2,256]{3,0,1,2:T(8,128)(2,1)S(1)}, u32[]{:S(2)}, u32[]{:S(2)}) collective-permute-start(bf16[16,1,2,256]{3,0,1,2:T(8,128)(2,1)S(1)} %collective-permute-done.1), channel_id=1, source_target_pairs={{0,496},{16,0},{32,16},{48,32},{64,48},{80,64},{96,80},{112,96},{1... | collective-permute-start | bytes 49160 | tf_op jit(solution)/shard_map/ppermute | solution.py:15
  178.2 6.7 %collective-permute-start.3 = (bf16[16,1,2,256]{3,0,1,2:T(8,128)(2,1)S(1)}, bf16[16,1,2,256]{3,0,1,2:T(8,128)(2,1)S(1)}, u32[]{:S(2)}, u32[]{:S(2)}) collective-permute-start(bf16[16,1,2,256]{3,0,1,2:T(8,128)(2,1)S(1)} %collective-permute-done.2), channel_id=1, source_target_pairs={{0,496},{16,0},{32,16},{48,32},{64,48},{80,64},{96,80},{112,96},{1... | collective-permute-start | bytes 49160 | tf_op jit(solution)/shard_map/ppermute | solution.py:15
  184.9 1.9 collective-permute-start.7
  186.9 2.6 add_convert_fusion.1
  189.5 3.2 %collective-permute-done.7 = bf16[16,1,2,256]{3,0,1,2:T(8,128)(2,1)S(1)} collective-permute-done((bf16[16,1,2,256]{3,0,1,2:T(8,128)(2,1)S(1)}, bf16[16,1,2,256]{3,0,1,2:T(8,128)(2,1)S(1)}, u32[]{:S(2)}, u32[]{:S(2)}) %collective-permute-start.7) | collective-permute-done | bytes 16416 | tf_op jit(solution)/shard_map/ppermute | solution.py:15
  192.7 2.6 add_convert_fusion
  196.2 6.2 %all-to-all-start.2 = ((bf16[16,16,2,2,256]{4,1,3,2,0:T(8,128)(2,1)}), bf16[16,16,2,2,256]{4,1,3,2,0:T(8,128)(2,1)S(1)}, u32[]{:S(2)}, u32[]{:S(2)}) async-start(bf16[16,16,2,2,256]{4,1,3,2,0:T(8,128)(2,1)} %stack.66), calls=%async_computation.3 | async-start | bytes 1048576 | tf_op jit(solution)/shard_map/all_to_all | solution.py:77
  202.4 17.3 %all-to-all-done.2 = bf16[16,16,2,2,256]{4,1,3,2,0:T(8,128)(2,1)S(1)} async-done(((bf16[16,16,2,2,256]{4,1,3,2,0:T(8,128)(2,1)}), bf16[16,16,2,2,256]{4,1,3,2,0:T(8,128)(2,1)S(1)}, u32[]{:S(2)}, u32[]{:S(2)}) %all-to-all-start.2) | async-done | bytes 524320 | tf_op jit(solution)/shard_map/all_to_all | solution.py:77
  219.8 49.6 %while.29 = (s32[]{:T(128)}, f32[2,2,1024]{2,1,0:T(2,128)S(1)}, s32[2,1024]{1,0:T(2,128)S(1)}, bf16[2,256,2,256]{3,1,2,0:T(8,128)(2,1)S(1)}, s32[2,1024]{1,0:T(2,128)S(1)}, /*index=5*/s32[]{:T(128)}) while((s32[]{:T(128)}, f32[2,2,1024]{2,1,0:T(2,128)S(1)}, s32[2,1024]{1,0:T(2,128)S(1)}, bf16[2,256,2,256]{3,1,2,0:T(8,128)(2,1)S(1)}, ...), condition=%wide.region_4.5_spmd, body=%wide.region_3.4_spmd.sunk | while | flops 19458 | bytes 1128533 | solution.py:181
  219.9 11.9 %copy.114 = bf16[1,256,2,256]{2,3,1,0:T(8,128)(2,1)} copy(bf16[1,256,2,256]{3,1,2,0:T(8,128)(2,1)S(1)} %constant_dynamic-slice_fusion.5) | data formatting | bytes 524288 | tf_op jit(solution)/shard_map/while/body/jit(dynamic_index_in_dim)/dynamic_slice | solution.py:181
  231.9 12.3 %gather_fusion = bf16[1024,2]{1,0:T(8,128)(2,1)S(1)} fusion(bf16[256,2,256]{1,2,0:T(8,128)(2,1)} %bitcast.205, s32[1024]{0:T(1024)S(1)} %bitcast.204), kind=kCustom, calls=%fused_computation.clone.1 | custom fusion | bytes 16384 | tf_op jit(solution)/shard_map/while/body/eval_jaxpr/gather | solution.py:46
  244.7 11.9 %copy.114 = bf16[1,256,2,256]{2,3,1,0:T(8,128)(2,1)} copy(bf16[1,256,2,256]{3,1,2,0:T(8,128)(2,1)S(1)} %constant_dynamic-slice_fusion.5) | data formatting | bytes 524288 | tf_op jit(solution)/shard_map/while/body/jit(dynamic_index_in_dim)/dynamic_slice | solution.py:181
  256.6 12.4 %gather_fusion = bf16[1024,2]{1,0:T(8,128)(2,1)S(1)} fusion(bf16[256,2,256]{1,2,0:T(8,128)(2,1)} %bitcast.205, s32[1024]{0:T(1024)S(1)} %bitcast.204), kind=kCustom, calls=%fused_computation.clone.1 | custom fusion | bytes 16384 | tf_op jit(solution)/shard_map/while/body/eval_jaxpr/gather | solution.py:46
  (103 shorter events, 46.3 us)
Async XLA Ops:
  6.5 96.4 %copy-start.1 = (f32[256,16]{0,1:T(8,128)S(1)}, f32[256,16]{0,1:T(8,128)}, u32[]{:S(2)}) copy-start(f32[256,16]{0,1:T(8,128)} %param.17) | copy-start | bytes 49156
  6.5 113.7 %copy-start.3 = (f32[4]{0:T(128)S(1)}, f32[4]{0:T(128)}, u32[]{:S(2)}) copy-start(f32[4]{0:T(128)} %param.18) | copy-start | bytes 52
  6.5 67.7 %reduce-scatter.2.cloned.1.call-start = ((), (), s32[]{:S(2)}) async-start(), calls=%async_computation.4 | async-start | bytes 557056 | tf_op jit(solution)/shard_map/reduce_scatter | solution.py:122
  10.6 0.8 copy-start
  10.6 133.8 %copy-start.4 = (f32[4]{0:T(128)S(1)}, f32[4]{0:T(128)}, u32[]{:S(2)}) copy-start(f32[4]{0:T(128)} %param.19) | copy-start | bytes 52
  79.9 15.2 %all-to-all-start = ((f32[16,1,1024]{2,1,0:T(1,128)}), f32[16,1,1024]{2,1,0:T(1,128)S(1)}, u32[]{:S(2)}, u32[]{:S(2)}) async-start(f32[16,1,1024]{2,1,0:T(1,128)} %reshape.204), calls=%async_computation.1 | async-start | bytes 131072 | tf_op jit(solution)/shard_map/all_to_all | solution.py:137
  116.8 12.7 %all-to-all-start.1 = ((f32[16,1,2048]{2,1,0:T(1,128)}), f32[16,1,2048]{2,1,0:T(1,128)S(1)}, u32[]{:S(2)}, u32[]{:S(2)}) async-start(f32[16,1,2048]{2,1,0:T(1,128)} %reshape.206), calls=%async_computation.2 | async-start | bytes 262144 | tf_op jit(solution)/shard_map/all_to_all | solution.py:151
  137.8 22.9 %collective-permute-start = (bf16[16,1,2,256]{3,0,1,2:T(8,128)(2,1)S(1)}, bf16[16,1,2,256]{3,0,1,2:T(8,128)(2,1)S(1)}, u32[]{:S(2)}, u32[]{:S(2)}) collective-permute-start(bf16[16,1,2,256]{3,0,1,2:T(8,128)(2,1)S(1)} %get-tuple-element.176), channel_id=1, source_target_pairs={{0,496},{16,0},{32,16},{48,32},{64,48},{80,64},{96,80},{112,96},{1... | collective-permute-start | bytes 49160 | tf_op jit(solution)/shard_map/ppermute | solution.py:15
  158.7 8.8 %collective-permute-start.4 = (bf16[16,1,2,256]{3,0,1,2:T(8,128)(2,1)S(1)}, bf16[16,1,2,256]{3,0,1,2:T(8,128)(2,1)S(1)}, u32[]{:S(2)}, u32[]{:S(2)}) collective-permute-start(bf16[16,1,2,256]{3,0,1,2:T(8,128)(2,1)S(1)} %get-tuple-element.177), channel_id=1, source_target_pairs={{0,16},{16,32},{32,48},{48,64},{64,80},{80,96},{96,112},{112,128},... | collective-permute-start | bytes 49160 | tf_op jit(solution)/shard_map/ppermute | solution.py:15
  160.7 8.8 %collective-permute-start.1 = (bf16[16,1,2,256]{3,0,1,2:T(8,128)(2,1)S(1)}, bf16[16,1,2,256]{3,0,1,2:T(8,128)(2,1)S(1)}, u32[]{:S(2)}, u32[]{:S(2)}) collective-permute-start(bf16[16,1,2,256]{3,0,1,2:T(8,128)(2,1)S(1)} %collective-permute-done), channel_id=1, source_target_pairs={{0,496},{16,0},{32,16},{48,32},{64,48},{80,64},{96,80},{112,96},{1... | collective-permute-start | bytes 49160 | tf_op jit(solution)/shard_map/ppermute | solution.py:15
  167.5 8.8 %collective-permute-start.5 = (bf16[16,1,2,256]{3,0,1,2:T(8,128)(2,1)S(1)}, bf16[16,1,2,256]{3,0,1,2:T(8,128)(2,1)S(1)}, u32[]{:S(2)}, u32[]{:S(2)}) collective-permute-start(bf16[16,1,2,256]{3,0,1,2:T(8,128)(2,1)S(1)} %collective-permute-done.4), channel_id=1, source_target_pairs={{0,16},{16,32},{32,48},{48,64},{64,80},{80,96},{96,112},{112,128},... | collective-permute-start | bytes 49160 | tf_op jit(solution)/shard_map/ppermute | solution.py:15
  169.5 8.7 %collective-permute-start.2 = (bf16[16,1,2,256]{3,0,1,2:T(8,128)(2,1)S(1)}, bf16[16,1,2,256]{3,0,1,2:T(8,128)(2,1)S(1)}, u32[]{:S(2)}, u32[]{:S(2)}) collective-permute-start(bf16[16,1,2,256]{3,0,1,2:T(8,128)(2,1)S(1)} %collective-permute-done.1), channel_id=1, source_target_pairs={{0,496},{16,0},{32,16},{48,32},{64,48},{80,64},{96,80},{112,96},{1... | collective-permute-start | bytes 49160 | tf_op jit(solution)/shard_map/ppermute | solution.py:15
  176.2 8.7 %collective-permute-start.6 = (bf16[16,1,2,256]{3,0,1,2:T(8,128)(2,1)S(1)}, bf16[16,1,2,256]{3,0,1,2:T(8,128)(2,1)S(1)}, u32[]{:S(2)}, u32[]{:S(2)}) collective-permute-start(bf16[16,1,2,256]{3,0,1,2:T(8,128)(2,1)S(1)} %collective-permute-done.5), channel_id=1, source_target_pairs={{0,16},{16,32},{32,48},{48,64},{64,80},{80,96},{96,112},{112,128},... | collective-permute-start | bytes 49160 | tf_op jit(solution)/shard_map/ppermute | solution.py:15
  178.2 8.7 %collective-permute-start.3 = (bf16[16,1,2,256]{3,0,1,2:T(8,128)(2,1)S(1)}, bf16[16,1,2,256]{3,0,1,2:T(8,128)(2,1)S(1)}, u32[]{:S(2)}, u32[]{:S(2)}) collective-permute-start(bf16[16,1,2,256]{3,0,1,2:T(8,128)(2,1)S(1)} %collective-permute-done.2), channel_id=1, source_target_pairs={{0,496},{16,0},{32,16},{48,32},{64,48},{80,64},{96,80},{112,96},{1... | collective-permute-start | bytes 49160 | tf_op jit(solution)/shard_map/ppermute | solution.py:15
  184.9 7.8 %collective-permute-start.7 = (bf16[16,1,2,256]{3,0,1,2:T(8,128)(2,1)S(1)}, bf16[16,1,2,256]{3,0,1,2:T(8,128)(2,1)S(1)}, u32[]{:S(2)}, u32[]{:S(2)}) collective-permute-start(bf16[16,1,2,256]{3,0,1,2:T(8,128)(2,1)S(1)} %collective-permute-done.6), channel_id=1, source_target_pairs={{0,16},{16,32},{32,48},{48,64},{64,80},{80,96},{96,112},{112,128},... | collective-permute-start | bytes 49160 | tf_op jit(solution)/shard_map/ppermute | solution.py:15
  196.2 23.5 %all-to-all-start.2 = ((bf16[16,16,2,2,256]{4,1,3,2,0:T(8,128)(2,1)}), bf16[16,16,2,2,256]{4,1,3,2,0:T(8,128)(2,1)S(1)}, u32[]{:S(2)}, u32[]{:S(2)}) async-start(bf16[16,16,2,2,256]{4,1,3,2,0:T(8,128)(2,1)} %stack.66), calls=%async_computation.3 | async-start | bytes 1048576 | tf_op jit(solution)/shard_map/all_to_all | solution.py:77
  219.8 49.7 %copy-start.2 = (f32[2,1,2,1024]{3,2,1,0:T(2,128)S(1)}, f32[2,1,2,1024]{3,2,1,0:T(2,128)}, u32[]{:S(2)}) copy-start(f32[2,1,2,1024]{3,2,1,0:T(2,128)} %param.14) | copy-start | bytes 49156
Sparse Core Ops, SparseCore 0:
  11.6 62.6 reduce-scatter.1
